TPU v7x, 256 devices: a whole 4x4x8 slice. The times are simulated.
256 devices in a mesh: seq: 32 (over y_lo, z, core), head: 8 (over x, y_hi).
Axes of the slice: x: 4, y: 4 (y_hi: 2, y_lo: 2; y = y_hi * 2 + y_lo), z: 8, core: 2. Of those that a mesh axis runs over, the one named last changes fastest.
Arguments:
- queries: bfloat16 [12288, 3072], P('seq', 'head'), may hold values from -56 to 56, as said below
- keys: bfloat16 [12288, 3072], P('seq', 'head'), may hold values from -4 to 4, as said below
- values: bfloat16 [12288, 3072], P('seq', 'head'), may hold values from -6 to 6
- out_weight: bfloat16 [3072, 3072], P('head'), may hold values from -0.109375 to 0.109375
- residual: bfloat16 [12288, 3072], P(('seq', 'head')), may hold values from -6 to 6
- gate: float32 [3072], replicated, may hold values from 0.5 to 2
Outputs:
- mixed: bfloat16 [12288, 3072], P(('seq', 'head'))
Inputs may be any that keep to these rules, and one draw needn't show every extreme that they name: `queries`: query entries of the attention. `keys`: key entries of the attention.
All inputs are finite; a program needn't handle non-finite values.
Results may differ from a plain program's by a relative error of at most 0.0075.
Values may be sent and summed in bfloat16 or wider, within the bound.
No kernel may reach another device: no remote copies, remote signals or barrier semaphores. Data moves between devices by JAX's collectives and lax.ppermute only.
A program may use at most 192 MiB of HBM per device.

v0:
```python
import jax
import jax.numpy as jnp
from jax import lax
from jax.sharding import PartitionSpec as P

HD = 128


def local(queries, keys, values, out_weight, residual, gate):
    tok_rows = queries.shape[0]
    heads_here = queries.shape[1] // HD
    scale = 1.0 / HD**0.5
    query_heads = queries.reshape(tok_rows, heads_here, HD)
    gathered = (
        lax.all_gather(keys, "seq", axis=0, tiled=True),
        lax.all_gather(values, "seq", axis=0, tiled=True),
    )
    running_max = jnp.full((heads_here, tok_rows), -1e30, jnp.float32)
    key_piece = gathered[0].reshape(-1, heads_here, HD)
    value_piece = gathered[1].reshape(-1, heads_here, HD)
    scores = (
        jnp.einsum("qhd,khd->hqk", query_heads, key_piece, preferred_element_type=jnp.float32)
        * scale
    )
    new_max = jnp.maximum(running_max, jnp.max(scores, axis=-1))
    expd = jnp.exp(scores - new_max[:, :, None])
    new_total = jnp.sum(expd, axis=-1)
    probs = expd.astype(jnp.bfloat16)
    added = jnp.einsum("hqk,khd->qhd", probs, value_piece, preferred_element_type=jnp.float32)
    final_state = (new_max, new_total, added)
    running_max, running_total, summed = final_state
    attention = (summed / jnp.transpose(running_total)[:, :, None]).astype(jnp.bfloat16)
    attention = attention.reshape(tok_rows, heads_here * HD)
    projected = lax.psum_scatter(
        jnp.dot(attention, out_weight, preferred_element_type=jnp.float32).astype(jnp.bfloat16),
        "head",
        scatter_dimension=0,
        tiled=True,
    ).astype(jnp.float32)
    return (residual.astype(jnp.float32) + gate * projected).astype(jnp.bfloat16)


def solution(mesh):
    placed = (
        P("seq", "head"),
        P("seq", "head"),
        P("seq", "head"),
        P("head", None),
        P(("seq", "head"), None),
        P(),
    )
    return jax.shard_map(
        local, mesh=mesh, in_specs=placed, out_specs=P(("seq", "head"), None), check_vma=False
    )
```

profile of v0, /device:TPU:2, one launch (start us, length us, event | category | flops | bytes accessed | tf_op | source)
XLA Modules:
  0.0 287.6 jit_solution(7186178622220679946)
XLA Ops:
  6.5 0.0 copy-start
  6.5 0.0 all-gather.3.cloned.1.call-start
  6.5 2.0 copy.10
  8.5 0.0 all-gather.3.cloned.1.call-update
  8.6 0.0 all-gather.5.cloned.1.call-start
  8.6 0.7 all-gather.5.cloned.1.call-update
  9.3 0.0 reduce-scatter.2.cloned.1.call-start
  9.4 1.2 copy.9
  10.5 75.2 %all-gather.3.cloned.1.call-done = bf16[12288,384]{0,1:T(8,128)(2,1)} async-done(((bf16[384,384]{0,1:T(8,128)(2,1)}), bf16[12288,384]{0,1:T(8,128)(2,1)}) %all-gather.3.cloned.1.call-update) | async-done | bytes 9437200 | tf_op jit(solution)/shard_map/all_gather | solution.py:15
  85.7 24.7 %multiply_reduce_fusion = (f32[3,384]{1,0:T(4,128)S(1)}, f32[3,384,12288]{2,1,0:T(8,128)}) fusion(bf16[384,3,128]{0,2,1:T(8,128)(2,1)S(1)} %bitcast.19, bf16[12288,3,128]{0,2,1:T(8,128)(2,1)} %bitcast.17), kind=kOutput, calls=%fused_computation.1 | convolution fusion | flops 3652189184 | bytes 66359808 | tf_op jit(solution)/shard_map/qhd,khd->hqk/dot_general | solution.py:22
  110.4 19.4 %fusion = f32[3,384]{1,0:T(4,128)S(1)} fusion(f32[3,384,12288]{2,1,0:T(8,128)} %get-tuple-element.6, f32[3,384]{1,0:T(4,128)S(1)} %broadcast_maximum_fusion), kind=kLoop, calls=%fused_computation.2 | loop fusion | flops 42466176 | bytes 56632320 | tf_op jit(solution)/shard_map/reduce_sum | solution.py:27
  129.8 29.4 %all-gather.5.cloned.1.call-done = bf16[12288,384]{1,0:T(8,128)(2,1)} async-done(((bf16[384,384]{1,0:T(8,128)(2,1)}), bf16[12288,384]{1,0:T(8,128)(2,1)}) %all-gather.5.cloned.1.call-update) | async-done | bytes 9437200 | tf_op jit(solution)/shard_map/all_gather | solution.py:16
  159.2 12.6 %copy.13 = bf16[12288,384]{0,1:T(8,128)(2,1)} copy(bf16[12288,384]{1,0:T(8,128)(2,1)} %all-gather.5.cloned.1.call-done) | data formatting | bytes 18874368 | tf_op jit(solution)/shard_map/all_gather | solution.py:16
  171.8 0.0 copy-start.1
  171.8 0.0 copy-start.2
  171.8 22.7 %fusion.12 = bf16[384,3,128]{0,2,1:T(8,128)(2,1)S(1)} fusion(bf16[12288,3,128]{0,2,1:T(8,128)(2,1)} %bitcast.16, f32[3,384,12288]{2,1,0:T(8,128)} %get-tuple-element.6, f32[3,384]{1,0:T(4,128)S(1)} %broadcast_maximum_fusion, f32[384,3]{0,1:T(4,128)S(1)} %bitcast.20), kind=kOutput, calls=%fused_computation.10 | convolution fusion | flops 3666640896 | bytes 66364416 | tf_op jit(solution)/shard_map/hqk,khd->qhd/dot_general | solution.py:29
  194.4 0.0 copy-done
  194.5 2.9 convolution_convert_fusion
  197.3 0.0 reduce-scatter.2.cloned.1.call-update
  197.3 82.0 %reduce-scatter.2.cloned.1.call-done = bf16[48,3072]{1,0:T(8,128)(2,1)} async-done(((bf16[384,3072]{1,0:T(8,128)(2,1)}), bf16[48,3072]{1,0:T(8,128)(2,1)}) %reduce-scatter.2.cloned.1.call-update) | async-done | bytes 294928 | tf_op jit(solution)/shard_map/reduce_scatter | solution.py:34
  279.3 0.0 copy-done.1
  279.3 0.0 copy-done.2
  279.3 1.8 add_convert_fusion
  (1 shorter events, 0.0 us)
Async XLA Ops:
  6.5 187.9 %copy-start = (bf16[384,3072]{1,0:T(8,128)(2,1)S(1)}, bf16[384,3072]{1,0:T(8,128)(2,1)}, u32[]{:S(2)}) copy-start(bf16[384,3072]{1,0:T(8,128)(2,1)} %param.9) | copy-start | bytes 7077892
  6.5 79.2 %all-gather.3.cloned.1.call-start = ((), (), s32[]{:S(2)}) async-start(), calls=%async_computation.1 | async-start | bytes 9732096 | tf_op jit(solution)/shard_map/all_gather | solution.py:15
  8.6 150.6 %all-gather.5.cloned.1.call-start = ((), (), s32[]{:S(2)}) async-start(), calls=%async_computation.2 | async-start | bytes 9732096 | tf_op jit(solution)/shard_map/all_gather | solution.py:16
  9.3 270.0 %reduce-scatter.2.cloned.1.call-start = ((), (), s32[]{:S(2)}) async-start(), calls=%async_computation.3 | async-start | bytes 2654208 | tf_op jit(solution)/shard_map/reduce_scatter | solution.py:34
  171.8 107.5 %copy-start.1 = (bf16[48,3072]{1,0:T(8,128)(2,1)S(1)}, bf16[48,3072]{1,0:T(8,128)(2,1)}, u32[]{:S(2)}) copy-start(bf16[48,3072]{1,0:T(8,128)(2,1)} %param.10) | copy-start | bytes 884740
  171.8 107.5 %copy-start.2 = (f32[3072]{0:T(1024)S(1)}, f32[3072]{0:T(1024)}, u32[]{:S(2)}) copy-start(f32[3072]{0:T(1024)} %param.11) | copy-start | bytes 36868
Sparse Core Ops, SparseCore 0:
  9.1 76.5 all-gather.2
  87.5 71.5 all-gather.4
  197.5 81.8 reduce-scatter.1
where the time goes:
time: 288 us
  waiting for transfers between devices  187 us (65%)
  matrix products  50.2 us (17%)
  other arithmetic  21.2 us (7%)
  local copies, waits for them, and re-layouts  15.8 us (5%)
  between operations  13.1 us (5%)
    reduce_scatter x1, waiting for transfers between devices, local(): lax.psum_scatter(jnp.dot(attention, out_weight, preferred_element_type=jn...  82 us
    all_gather x1, waiting for transfers between devices, local(): lax.all_gather(keys, 'seq', axis=0, tiled=True)  75.2 us
    all_gather x1, waiting for transfers between devices, local(): lax.all_gather(values, 'seq', axis=0, tiled=True)  29.4 us
    dot_general x1, matrix products, local(): jnp.einsum('qhd,khd->hqk', query_heads, key_piece, preferred_element_type...  24.7 us
    dot_general x1, matrix products, local(): jnp.einsum('hqk,khd->qhd', probs, value_piece, preferred_element_type=jnp...  22.7 us
    reduce_sum x1, other arithmetic, local(): new_total = jnp.sum(expd, axis=-1)  19.4 us
    all_gather x1, local copies, waits for them, and re-layouts, local(): lax.all_gather(values, 'seq', axis=0, tiled=True)  12.6 us
  transfers between devices with their start and end apart: 3, of which 3 were waited for; matrix products, arithmetic and copies ran while one was open for 16% of the time, Pallas kernels for 0%

commit v1 on v0

--- a/solution.py
+++ b/solution.py
@@ -2,8 +2,18 @@
 import jax.numpy as jnp
 from jax import lax
 from jax.sharding import PartitionSpec as P
+from jax.lax import all_to_all, axis_size
 
 HD = 128
+
+
+def link_the_threads(xin):
+    return jnp.concatenate(
+        all_to_all(
+            jnp.stack(axis_size("seq") * [xin]), axis_name="seq", split_axis=0, concat_axis=0
+        ),
+        axis=0,
+    )
 
 
 def local(queries, keys, values, out_weight, residual, gate):
@@ -11,10 +21,7 @@
     heads_here = queries.shape[1] // HD
     scale = 1.0 / HD**0.5
     query_heads = queries.reshape(tok_rows, heads_here, HD)
-    gathered = (
-        lax.all_gather(keys, "seq", axis=0, tiled=True),
-        lax.all_gather(values, "seq", axis=0, tiled=True),
-    )
+    gathered = (lax.all_gather(keys, "seq", axis=0, tiled=True), link_the_threads(values))
     running_max = jnp.full((heads_here, tok_rows), -1e30, jnp.float32)
     key_piece = gathered[0].reshape(-1, heads_here, HD)
     value_piece = gathered[1].reshape(-1, heads_here, HD)

time: 288 us -> 449 us (1.56)
  waiting for transfers between devices: 187 us -> 319 us
  local copies, waits for them, and re-layouts: 15.8 us -> 35.4 us
  starting transfers between devices: 0.08 us -> 10 us
    all_gather x1, waiting for transfers between devices: 75.2 us -> 188 us  [local(): lax.all_gather(keys, 'seq', axis=0, tiled=True)]
    all_to_all x0 -> x1, waiting for transfers between devices: none -> 41.8 us  [link_the_threads(): all_to_all(jnp.stack(axis_size('seq') * [xin]), axis_name='seq', split_ax...]
    all_gather x1 -> x0, waiting for transfers between devices: 29.4 us -> none  [local(): lax.all_gather(values, 'seq', axis=0, tiled=True)]
    another operation x0 -> x2, local copies, waits for them, and re-layouts: none -> 19.2 us  [the longest x1 14.1 us: local(): value_piece = gathered[1].reshape(-1, heads_here, HD)]
    all_to_all x0 -> x1, local copies, waits for them, and re-layouts: none -> 12.8 us  [link_the_threads(): all_to_all(jnp.stack(axis_size('seq') * [xin]), axis_name='seq', split_ax...]
    all_gather x1 -> x0, local copies, waits for them, and re-layouts: 12.6 us -> none  [local(): lax.all_gather(values, 'seq', axis=0, tiled=True)]
    all_to_all x0 -> x1, starting transfers between devices: none -> 9.98 us  [link_the_threads(): all_to_all(jnp.stack(axis_size('seq') * [xin]), axis_name='seq', split_ax...]
    reduce_scatter x1, waiting for transfers between devices: 82 us -> 88.8 us  [local(): lax.psum_scatter(jnp.dot(attention, out_weight, preferred_element_type=jn...]
  transfers between devices with their start and end apart: 3 -> 3, of which waited for: 3 -> 3; matrix products, arithmetic and copies ran while one was open for 16% -> 7% of each run, Pallas kernels for 0% -> 0%
where the time goes in v1:
time: 449 us; the launch traced here: 448 us
  waiting for transfers between devices  319 us (71%)
  matrix products  50 us (11%)
  local copies, waits for them, and re-layouts  35.4 us (8%)
  other arithmetic  20.4 us (5%)
  between operations  13.5 us (3%)
  starting transfers between devices  10 us (2%)
    all_gather x1, waiting for transfers between devices, local(): lax.all_gather(keys, 'seq', axis=0, tiled=True)  188 us
    reduce_scatter x1, waiting for transfers between devices, local(): lax.psum_scatter(jnp.dot(attention, out_weight, preferred_element_type=jn...  88.8 us
    all_to_all x1, waiting for transfers between devices, link_the_threads(): all_to_all(jnp.stack(axis_size('seq') * [xin]), axis_name='seq', split_ax...  41.8 us
    dot_general x1, matrix products, local(): jnp.einsum('qhd,khd->hqk', query_heads, key_piece, preferred_element_type...  24.2 us
    dot_general x1, matrix products, local(): jnp.einsum('hqk,khd->qhd', probs, value_piece, preferred_element_type=jnp...  22.9 us
    reduce_sum x1, other arithmetic, local(): new_total = jnp.sum(expd, axis=-1)  18.6 us
    another operation x1, local copies, waits for them, and re-layouts, local(): value_piece = gathered[1].reshape(-1, heads_here, HD)  14.1 us
    all_to_all x1, local copies, waits for them, and re-layouts, link_the_threads(): all_to_all(jnp.stack(axis_size('seq') * [xin]), axis_name='seq', split_ax...  12.8 us
  transfers between devices with their start and end apart: 3, of which 3 were waited for; matrix products, arithmetic and copies ran while one was open for 7% of the time, Pallas kernels for 0%

profile of v1, /device:TPU:2, one launch (start us, length us, event | category | flops | bytes accessed | tf_op | source)
XLA Modules:
  0.0 448.2 jit_solution(4885025949913287093)
XLA Ops:
  6.5 0.0 copy-start
  6.5 0.0 copy-start.2
  6.5 0.0 all-gather.2.cloned.1.call-start
  6.5 2.0 copy.15
  8.5 0.0 all-gather.2.cloned.1.call-update
  8.6 1.2 copy.18
  9.7 5.1 %stack.2 = bf16[32,384,384]{1,2,0:T(8,128)(2,1)} broadcast(bf16[384,384]{0,1:T(8,128)(2,1)S(1)} %copy.18), dimensions={1,2} | broadcast | bytes 9732096 | tf_op jit(solution)/shard_map/stack | solution.py:13
  14.8 10.0 %all-to-all-start = ((bf16[32,384,384]{1,2,0:T(8,128)(2,1)}), bf16[32,384,384]{1,2,0:T(8,128)(2,1)}, u32[]{:S(2)}, u32[]{:S(2)}) async-start(bf16[32,384,384]{1,2,0:T(8,128)(2,1)} %stack.2), calls=%async_computation | async-start | bytes 18874368 | tf_op jit(solution)/shard_map/all_to_all | solution.py:12
  24.8 0.0 reduce-scatter.2.cloned.1.call-start
  24.9 0.0 copy-done.2
  24.9 0.2 copy.14
  25.1 188.3 %all-gather.2.cloned.1.call-done = bf16[12288,384]{0,1:T(8,128)(2,1)} async-done(((bf16[384,384]{0,1:T(8,128)(2,1)}), bf16[12288,384]{0,1:T(8,128)(2,1)}) %all-gather.2.cloned.1.call-update) | async-done | bytes 9437200 | tf_op jit(solution)/shard_map/all_gather | solution.py:24
  213.4 24.2 %multiply_reduce_fusion = (f32[3,384]{1,0:T(4,128)S(1)}, f32[3,384,12288]{2,1,0:T(8,128)}) fusion(bf16[384,3,128]{0,2,1:T(8,128)(2,1)S(1)} %bitcast.19, bf16[12288,3,128]{0,2,1:T(8,128)(2,1)} %bitcast.17), kind=kOutput, calls=%fused_computation.1 | convolution fusion | flops 3652189184 | bytes 66359808 | tf_op jit(solution)/shard_map/qhd,khd->hqk/dot_general | solution.py:29
  237.6 41.8 %all-to-all-done = bf16[32,384,384]{1,2,0:T(8,128)(2,1)} async-done(((bf16[32,384,384]{1,2,0:T(8,128)(2,1)}), bf16[32,384,384]{1,2,0:T(8,128)(2,1)}, u32[]{:S(2)}, u32[]{:S(2)}) %all-to-all-start) | async-done | bytes 9437216 | tf_op jit(solution)/shard_map/all_to_all | solution.py:12
  279.5 12.8 %copy.19 = bf16[32,384,384]{1,0,2:T(8,128)(2,1)} copy(bf16[32,384,384]{1,2,0:T(8,128)(2,1)} %all-to-all-done) | data formatting | bytes 18874368 | tf_op jit(solution)/shard_map/all_to_all | solution.py:12
  292.2 14.1 %reshape_reshape.3 = bf16[12288,3,128]{0,2,1:T(8,128)(2,1)} reshape(bf16[32,384,384]{1,0,2:T(8,128)(2,1)} %copy.19) | data formatting | bytes 18874368 | tf_op jit(solution)/shard_map/reshape;reshape | solution.py:27
  306.4 18.6 %fusion = f32[3,384]{1,0:T(4,128)S(1)} fusion(f32[3,384,12288]{2,1,0:T(8,128)} %get-tuple-element.6, f32[3,384]{1,0:T(4,128)S(1)} %broadcast_maximum_fusion), kind=kLoop, calls=%fused_computation.2 | loop fusion | flops 42466176 | bytes 56632320 | tf_op jit(solution)/shard_map/reduce_sum | solution.py:34
  325.0 0.0 copy-start.1
  325.0 0.0 copy-start.3
  325.0 22.9 %fusion.12 = bf16[384,3,128]{0,2,1:T(8,128)(2,1)S(1)} fusion(bf16[12288,3,128]{0,2,1:T(8,128)(2,1)} %reshape_reshape.3, f32[3,384,12288]{2,1,0:T(8,128)} %get-tuple-element.6, f32[3,384]{1,0:T(4,128)S(1)} %broadcast_maximum_fusion, f32[384,3]{0,1:T(4,128)S(1)} %bitcast.20), kind=kOutput, calls=%fused_computation.10 | convolution fusion | flops 3666640896 | bytes 66364416 | tf_op jit(solution)/shard_map/hqk,khd->qhd/dot_general | solution.py:36
  347.9 0.0 copy-done
  347.9 2.9 convolution_convert_fusion
  350.8 0.0 reduce-scatter.2.cloned.1.call-update
  350.8 88.8 %reduce-scatter.2.cloned.1.call-done = bf16[48,3072]{1,0:T(8,128)(2,1)} async-done(((bf16[384,3072]{1,0:T(8,128)(2,1)}), bf16[48,3072]{1,0:T(8,128)(2,1)}) %reduce-scatter.2.cloned.1.call-update) | async-done | bytes 294928 | tf_op jit(solution)/shard_map/reduce_scatter | solution.py:41
  439.6 0.0 copy-done.1
  439.6 0.0 copy-done.3
  439.6 1.8 add_convert_fusion
  (1 shorter events, 0.0 us)
Async XLA Ops:
  6.5 341.4 %copy-start = (bf16[384,3072]{1,0:T(8,128)(2,1)S(1)}, bf16[384,3072]{1,0:T(8,128)(2,1)}, u32[]{:S(2)}) copy-start(bf16[384,3072]{1,0:T(8,128)(2,1)} %param.9) | copy-start | bytes 7077892
  6.5 18.3 %copy-start.2 = (bf16[384,384]{1,0:T(8,128)(2,1)S(1)}, bf16[384,384]{1,0:T(8,128)(2,1)}, u32[]{:S(2)}) copy-start(bf16[384,384]{1,0:T(8,128)(2,1)} %param.6) | copy-start | bytes 884740
  6.5 206.9 %all-gather.2.cloned.1.call-start = ((), (), s32[]{:S(2)}) async-start(), calls=%async_computation.2 | async-start | bytes 9732096 | tf_op jit(solution)/shard_map/all_gather | solution.py:24
  14.8 264.6 %all-to-all-start = ((bf16[32,384,384]{1,2,0:T(8,128)(2,1)}), bf16[32,384,384]{1,2,0:T(8,128)(2,1)}, u32[]{:S(2)}, u32[]{:S(2)}) async-start(bf16[32,384,384]{1,2,0:T(8,128)(2,1)} %stack.2), calls=%async_computation | async-start | bytes 18874368 | tf_op jit(solution)/shard_map/all_to_all | solution.py:12
  24.8 414.8 %reduce-scatter.2.cloned.1.call-start = ((), (), s32[]{:S(2)}) async-start(), calls=%async_computation.3 | async-start | bytes 2654208 | tf_op jit(solution)/shard_map/reduce_scatter | solution.py:41
  325.0 114.6 %copy-start.1 = (bf16[48,3072]{1,0:T(8,128)(2,1)S(1)}, bf16[48,3072]{1,0:T(8,128)(2,1)}, u32[]{:S(2)}) copy-start(bf16[48,3072]{1,0:T(8,128)(2,1)} %param.10) | copy-start | bytes 884740
  325.0 114.6 %copy-start.3 = (f32[3072]{0:T(1024)S(1)}, f32[3072]{0:T(1024)}, u32[]{:S(2)}) copy-start(f32[3072]{0:T(1024)} %param.11) | copy-start | bytes 36868
Sparse Core Ops, SparseCore 0:
  9.1 204.2 all-gather.1
  350.9 88.6 reduce-scatter.1
